TPU v7x, 32 devices: a whole 2x2x4 slice. The times are simulated.
32 devices in a mesh: grp: 2 (over y), wide: 8 (over z, x), narrow: 2 (over core).
Axes of the slice: x: 2, y: 2, z: 4, core: 2. Of those that a mesh axis runs over, the one named last changes fastest.
Arguments:
- denoised: float32 [4, 512, 512], P('grp', 'wide', 'narrow'), parts along dimension 0, may hold values from -6 to 6
- clean_volume: float32 [4, 512, 512], P('grp', 'wide', 'narrow'), parts along dimension 0, may hold values from -6 to 6
- weight: float32 [512, 512], P(('wide', 'narrow')), may hold values from 0.1 to 2
- act_in: bfloat16 [64, 4, 512, 512], P(None, 'grp', 'wide', 'narrow'), parts along dimension 1, may hold values from -6 to 6
- act_mid: bfloat16 [64, 4, 512, 512], P(None, 'grp', 'wide', 'narrow'), parts along dimension 1, as said below
- w_first: bfloat16 [27, 64, 64], replicated, may hold values from -0.15625 to 0.15625
- w_second: bfloat16 [27, 64], replicated, may hold values from -0.15625 to 0.15625
Outputs:
- grad_in: bfloat16 [64, 4, 512, 512], P(None, 'grp', 'wide', 'narrow'), parts along dimension 1
- grad_first: float32 [54, 64, 64], P('grp'), parts along dimension 0
- grad_second: float32 [54, 64], P('grp'), parts along dimension 0
There are 2 independent parts, one for each index of `grp`. A program takes and returns all parts, laid end to end along the dimension named above; an argument that names none is the same for every part. Nothing has to cross between parts.
Inputs may be any that keep to these rules, and one draw needn't show every extreme that they name: act_mid is a rectifier's output: non-negative, with many zeros.
All inputs are finite; a program needn't handle non-finite values.
Results may differ from a plain program's by a relative error of at most 0.0058.
Values may be sent and summed in bfloat16 or wider, within the bound.
No kernel may reach another device: no remote copies, remote signals or barrier semaphores. Data moves between devices by JAX's collectives and lax.ppermute only.
A program may use at most 320 MiB of HBM per device.

v0:
```python
import jax
import jax.numpy as jnp
from jax import lax
from jax.sharding import PartitionSpec as P

two_pi = 6.283185307179586
highest = lax.Precision.HIGHEST


def with_halo(x, sides, width):
    for axis, dim in sides:
        devices, length = (lax.axis_size(axis), x.shape[dim])
        up = [(i, (i + 1) % devices) for i in range(devices - 1)]
        down = [(j, i) for i, j in up]
        last = lax.slice_in_dim(x, length - width, length, axis=dim)
        first = lax.slice_in_dim(x, 0, width, axis=dim)
        before = lax.ppermute(last, axis, up)
        after = lax.ppermute(first, axis, down)
        x = jnp.concatenate([before, x, after], axis=dim)
    return x


def phase_table(left_index, right_index, length):
    product = left_index[:, None] * right_index[None, :] % length
    angles = product.astype(jnp.float32) * (two_pi / length)
    return (jnp.cos(angles), jnp.sin(angles))


def shifted_windows(padded, slices, rows_x, cols_y, taps_list):
    windows = []
    for tap_index in taps_list:
        step_z = tap_index // 9 - 1
        step_x = tap_index // 3 % 3 - 1
        step_y = tap_index % 3 - 1
        windows.append(
            padded[
                ...,
                1 - step_z : 1 - step_z + slices,
                1 - step_x : 1 - step_x + rows_x,
                1 - step_y : 1 - step_y + cols_y,
            ]
        )
    return jnp.stack(windows, axis=0)


def shards(denoised, clean_volume, weight, act_in, act_mid, w_first, w_second):
    wide_count = lax.axis_size("wide")
    narrow_count = lax.axis_size("narrow")
    slices, rows_x, half_cols = denoised.shape
    total_y = half_cols * narrow_count
    total_x = rows_x * wide_count
    kept_cols = half_cols // wide_count
    narrow_index = lax.axis_index("narrow")
    error_field = denoised - clean_volume
    columns = lax.iota(jnp.int32, total_y)
    frequency = (
        columns % half_cols // kept_cols * narrow_count + columns // half_cols
    ) * kept_cols + columns % kept_cols
    own_rows = narrow_index * half_cols + lax.iota(jnp.int32, half_cols)
    cos_y, sin_y = phase_table(own_rows, frequency, total_y)
    part_real = jnp.einsum("zxy,yc->zxc", error_field, cos_y, precision=highest)
    part_imag = -jnp.einsum("zxy,yc->zxc", error_field, sin_y, precision=highest)
    spec_real, spec_imag = (
        lax.psum_scatter(part_real, "narrow", scatter_dimension=2, tiled=True),
        lax.psum_scatter(part_imag, "narrow", scatter_dimension=2, tiled=True),
    )
    positions = lax.iota(jnp.int32, total_x)
    cos_x, sin_x = phase_table(positions, positions, total_x)
    pieces = (
        lax.all_to_all(
            spec_real.reshape(slices, rows_x, wide_count, kept_cols),
            "wide",
            split_axis=2,
            concat_axis=1,
            tiled=True,
        ),
        lax.all_to_all(
            spec_imag.reshape(slices, rows_x, wide_count, kept_cols),
            "wide",
            split_axis=2,
            concat_axis=1,
            tiled=True,
        ),
    )
    item_count = pieces[0].shape[0]
    in_real = pieces[0].reshape(item_count, total_x, kept_cols)
    in_imag = pieces[1].reshape(item_count, total_x, kept_cols)
    four_real = jnp.einsum("mxk,xq->mkq", in_real, cos_x, precision=highest) + jnp.einsum(
        "mxk,xq->mkq", in_imag, sin_x, precision=highest
    )
    four_imag = jnp.einsum("mxk,xq->mkq", in_imag, cos_x, precision=highest) - jnp.einsum(
        "mxk,xq->mkq", in_real, sin_x, precision=highest
    )
    weighted_real = weight * four_real
    weighted_imag = weight * four_imag
    out_real = jnp.einsum("mkq,qx->mxk", weighted_real, cos_x, precision=highest) - jnp.einsum(
        "mkq,qx->mxk", weighted_imag, sin_x, precision=highest
    )
    out_imag = jnp.einsum("mkq,qx->mxk", weighted_imag, cos_x, precision=highest) + jnp.einsum(
        "mkq,qx->mxk", weighted_real, sin_x, precision=highest
    )
    back_real = lax.all_to_all(
        out_real.reshape(item_count, wide_count, rows_x, kept_cols),
        "wide",
        split_axis=1,
        concat_axis=3,
        tiled=True,
    ).reshape(item_count, rows_x, half_cols)
    back_imag = lax.all_to_all(
        out_imag.reshape(item_count, wide_count, rows_x, kept_cols),
        "wide",
        split_axis=1,
        concat_axis=3,
        tiled=True,
    ).reshape(item_count, rows_x, half_cols)
    local_cols = lax.iota(jnp.int32, half_cols)
    own_freq = (
        local_cols // kept_cols * narrow_count + narrow_index
    ) * kept_cols + local_cols % kept_cols
    cos_back, sin_back = phase_table(own_freq, columns, total_y)
    part_term = jnp.einsum("zxc,cy->zxy", back_real, cos_back, precision=highest) - jnp.einsum(
        "zxc,cy->zxy", back_imag, sin_back, precision=highest
    )
    field_real = lax.psum_scatter(part_term, "narrow", scatter_dimension=2, tiled=True)
    grad_noise = (field_real * (-2.0 / (total_x * total_y))).astype(jnp.bfloat16)
    noise_rim = with_halo(grad_noise, (("wide", 1), ("narrow", 2)), 1)
    noise_pad = jnp.pad(noise_rim, ((1, 1), (0, 0), (0, 0)))
    noise_windows = shifted_windows(noise_pad, slices, rows_x, half_cols, range(27))
    grad_mid = jnp.einsum(
        "tc,tzxy->czxy", w_second, noise_windows, preferred_element_type=jnp.float32
    )
    masked = jnp.where(act_mid > 0, grad_mid, 0.0).astype(jnp.bfloat16)
    masked_rim = with_halo(masked, (("wide", 2), ("narrow", 3)), 1)
    grad_second = jnp.einsum(
        "czxy,tzxy->tc", act_mid, noise_windows, preferred_element_type=jnp.float32
    )
    masked_pad = jnp.pad(masked_rim, ((0, 0), (1, 1), (0, 0), (0, 0)))
    channels = act_in.shape[0]
    grad_in = jnp.zeros(act_in.shape, jnp.float32)
    first_parts = []
    for plane_index in range(9):
        stacked = shifted_windows(
            masked_pad, slices, rows_x, half_cols, [plane_index, plane_index + 9, plane_index + 18]
        )
        first_parts.append(
            jnp.einsum("izxy,dozxy->dio", act_in, stacked, preferred_element_type=jnp.float32)
        )
        grad_in = grad_in + jnp.einsum(
            "dio,dozxy->izxy", w_first[plane_index::9], stacked, preferred_element_type=jnp.float32
        )
    grad_first = jnp.stack(first_parts, axis=1).reshape(27, channels, channels)
    grad_first, grad_second = lax.psum((grad_first, grad_second), ("wide", "narrow"))
    return (grad_in.astype(jnp.bfloat16), grad_first, grad_second)


def solution(mesh):
    placed = (
        P("grp", "wide", "narrow"),
        P("grp", "wide", "narrow"),
        P(("wide", "narrow"), None),
        P(None, "grp", "wide", "narrow"),
        P(None, "grp", "wide", "narrow"),
        P(),
        P(),
    )
    return jax.shard_map(
        shards,
        mesh=mesh,
        in_specs=placed,
        out_specs=(P(None, "grp", "wide", "narrow"), P("grp", None, None), P("grp", None)),
        check_vma=False,
    )
```

profile of v0, /device:TPU:0, one launch (start us, length us, event | category | flops | bytes accessed | tf_op | source)
XLA Modules:
  0.0 590.2 jit_solution(6544291308981167660)
XLA Ops:
  15.5 6.4 %reduce-scatter.4.cloned.1.call-done = f32[2,64,256]{2,1,0:T(8,128)} async-done(((f32[2,64,512]{2,1,0:T(8,128)}), f32[2,64,256]{2,1,0:T(8,128)}) %reduce-scatter.4.cloned.1.call-update) | async-done | bytes 131088 | tf_op jit(solution)/shard_map/reduce_scatter | solution.py:64
  23.8 5.7 all-to-all-start
  98.9 6.0 %all-to-all-done.3 = f32[8,1,4096]{2,1,0:T(1,128)S(1)} async-done(((f32[8,1,4096]{2,1,0:T(1,128)}), f32[8,1,4096]{2,1,0:T(1,128)S(1)}, u32[]{:S(2)}, u32[]{:S(2)}) %all-to-all-start.3) | async-done | bytes 131104 | tf_op jit(solution)/shard_map/all_to_all | solution.py:109
  147.6 6.3 %fusion.100 = f32[27,64]{1,0:T(8,128)S(1)} fusion(bf16[64,2,64,256]{3,2,1,0:T(8,128)(2,1)S(1)} %copy-done.27, bf16[27,2,64,256]{3,2,1,0:T(8,128)(2,1)S(1)} %constant_dynamic-update-slice_fusion), kind=kOutput, calls=%fused_computation.124 | convolution fusion | flops 113246208 | bytes 5970688 | tf_op jit(solution)/shard_map/czxy,tzxy->tc/dot_general | solution.py:134
  154.0 60.0 %psum.15 = f32[27,64]{1,0:T(8,128)} all-reduce(f32[27,64]{1,0:T(8,128)S(1)} %fusion.100), channel_id=1, replica_groups=mesh['grp'=2,'wide'=8,'narrow'=2] {'wide','narrow'}, use_global_device_ids=true, to_apply=%region_4.5 | all-reduce | flops 1728 | bytes 13824 | tf_op jit(solution)/shard_map/psum | solution.py:152
  227.9 5.8 fusion.27
  242.7 8.2 %pad_maximum_fusion.9 = (bf16[64,2,66,257]{3,0,2,1:T(8,128)(2,1)S(1)}, bf16[64,2,66,257]{3,0,2,1:T(8,128)(2,1)S(1)}) fusion(bf16[64,2,66,1]{3,0,2,1:T(8,128)(2,1)} %copy.104, bf16[64,2,1,256]{3,0,2,1:T(8,128)(2,1)S(1)} %collective-permute-done.5, bf16[64,2,64,256]{3,0,2,1:T(8,128)(2,1)} %copy-done.2, bf16[64,2,1,256]{3,0,2,1:T(8,128)(2,1)S(1)} %collective-permute-done.4, ...), kind=kLoop, calls=%fused_computation.30 | loop fusion | flops 34738176 | bytes 13043712 | tf_op jit(solution)/shard_map/concatenate | solution.py:19
  250.9 9.2 %slice_bitcast_fusion.22 = (bf16[1,64,2,64,256]{4,1,3,2,0:T(8,128)(2,1)}, bf16[1,64,2,64,256]{4,1,3,2,0:T(8,128)(2,1)}, bf16[1,64,2,64,256]{4,1,3,2,0:T(8,128)(2,1)}) fusion(bf16[64,2,66,257]{3,0,2,1:T(8,128)(2,1)S(1)} %get-tuple-element.36), kind=kLoop, calls=%fused_computation.77 | loop fusion | bytes 25165824 | tf_op jit(solution)/shard_map/stack | solution.py:43
  260.1 8.9 %select_maximum_fusion = bf16[64,4,66,258]{3,0,2,1:T(8,128)(2,1)} fusion(bf16[64,2,66,1]{3,0,2,1:T(8,128)(2,1)} %copy.104, bf16[64,2,66,1]{3,0,2,1:T(8,128)(2,1)S(1)} %copy-done.4, bf16[64,2,1,256]{3,0,2,1:T(8,128)(2,1)S(1)} %collective-permute-done.5, bf16[64,2,64,256]{3,0,2,1:T(8,128)(2,1)S(1)} %copy-done.3, ...), kind=kLoop, calls=%fused_computation.3 | loop fusion | flops 78465024 | bytes 13077504 | tf_op jit(solution)/shard_map/concatenate | solution.py:19
  269.1 64.1 %slice_bitcast_fusion.23 = (bf16[1,64,2,64,256]{4,1,3,2,0:T(8,128)(2,1)}, bf16[1,64,2,64,256]{4,1,3,2,0:T(8,128)(2,1)}, bf16[1,64,2,64,256]{4,1,3,2,0:T(8,128)(2...) fusion(bf16[64,4,66,258]{3,0,2,1:T(8,128)(2,1)} %select_maximum, ...), kind=kLoop, calls=%fused_computation.78 | loop fusion | bytes 150994944 | tf_op jit(solution)/shard_map/stack | solution.py:43
  333.2 15.3 %fusion.49 = f32[3,9,64,64]{2,3,0,1:T(8,128)} fusion(bf16[1,64,2,64,256]{4,1,3,2,0:T(8,128)(2,1)} %get-tuple-element.28, bf16[1,64,2,64,256]{4,1,3,2,0:T(8,128)(2,1)} %get-tuple-element.30, bf16[1,64,2,64,256]{4,1,3,2,0:T(8,128)(2,1)} %get-tuple-element.12, bf16[64,2,64,256,1]{3,2,1,0,4:T(8,128)(2,1)} %bitcast.559), kind=kOutput, calls=%fused_computation.107 | convolution fusion | flops 817889280 | bytes 16875520 | tf_op jit(solution)/shard_map/izxy,dozxy->dio/dot_general | solution.py:146
  348.6 8.5 %fusion.25 = f32[2,64,256,64,1]{2,3,1,0,4:T(8,128)} fusion(bf16[1,64,2,64,256]{4,1,3,2,0:T(8,128)(2,1)} %get-tuple-element.28, bf16[1,64,2,64,256]{4,1,3,2,0:T(8,128)(2,1)} %get-tuple-element.30, bf16[1,64,2,64,256]{4,1,3,2,0:T(8,128)(2,1)} %get-tuple-element.12, bf16[27,64,64]{2,1,0:T(8,128)(2,1)S(1)} %copy-done.29), kind=kOutput, calls=%fused_computation.49 | convolution fusion | flops 843055104 | bytes 21020672 | tf_op jit(solution)/shard_map/dio,dozxy->izxy/dot_general | solution.py:148
  365.0 9.2 %fusion.55 = f32[3,9,64,64]{2,3,0,1:T(8,128)} fusion(f32[3,9,64,64]{2,3,0,1:T(8,128)} %fusion.49, bf16[1,64,2,64,256]{4,1,3,2,0:T(8,128)(2,1)S(1)} %copy-done.21, bf16[1,64,2,64,256]{4,1,3,2,0:T(8,128)(2,1)S(1)} %copy-done.10, bf16[1,64,2,64,256]{4,1,3,2,0:T(8,128)(2,1)S(1)} %copy-done.22, bf16[64,2,64,256,1]{3,2,1,0,4:T(8,128)(2,1)} %bitcast.560), kind=kOutput, calls=%fused_computation.109 | convolution fusion | flops 817889280 | bytes 16875520 | tf_op jit(solution)/shard_map/izxy,dozxy->dio/dot_general | solution.py:146
  387.2 10.4 %fusion.61 = f32[3,9,64,64]{2,3,0,1:T(8,128)} fusion(f32[3,9,64,64]{2,3,0,1:T(8,128)} %fusion.55, bf16[1,64,2,64,256]{4,1,3,2,0:T(8,128)(2,1)S(1)} %copy-done.19, bf16[1,64,2,64,256]{4,1,3,2,0:T(8,128)(2,1)} %copy-done.26, bf16[1,64,2,64,256]{4,1,3,2,0:T(8,128)(2,1)S(1)} %copy-done.20, bf16[64,2,64,256,1]{3,2,1,0,4:T(8,128)(2,1)} %bitcast.561), kind=kOutput, calls=%fused_computation.111 | convolution fusion | flops 817889280 | bytes 16875520 | tf_op jit(solution)/shard_map/izxy,dozxy->dio/dot_general | solution.py:146
  397.6 6.5 %fusion.19 = f32[2,64,256,64,1]{2,3,1,0,4:T(8,128)} fusion(bf16[1,64,2,64,256]{4,1,3,2,0:T(8,128)(2,1)S(1)} %copy-done.17, bf16[1,64,2,64,256]{4,1,3,2,0:T(8,128)(2,1)} %get-tuple-element.32, bf16[1,64,2,64,256]{4,1,3,2,0:T(8,128)(2,1)S(1)} %copy-done.18, bf16[27,64,64]{2,1,0:T(8,128)(2,1)S(1)} %copy-done.29), kind=kOutput, calls=%fused_computation.43 | convolution fusion | flops 843055104 | bytes 21020672 | tf_op jit(solution)/shard_map/dio,dozxy->izxy/dot_general | solution.py:148
  404.2 10.4 %fusion.67 = f32[3,9,64,64]{2,3,0,1:T(8,128)} fusion(f32[3,9,64,64]{2,3,0,1:T(8,128)} %fusion.61, bf16[1,64,2,64,256]{4,1,3,2,0:T(8,128)(2,1)S(1)} %copy-done.17, bf16[1,64,2,64,256]{4,1,3,2,0:T(8,128)(2,1)} %get-tuple-element.32, bf16[1,64,2,64,256]{4,1,3,2,0:T(8,128)(2,1)S(1)} %copy-done.18, bf16[64,2,64,256,1]{3,2,1,0,4:T(8,128)(2,1)} %bitcast.562), kind=kOutput, calls=%fused_computation.113 | convolution fusion | flops 817889280 | bytes 16875520 | tf_op jit(solution)/shard_map/izxy,dozxy->dio/dot_general | solution.py:146
  420.0 9.3 %fusion.73 = f32[3,9,64,64]{2,3,0,1:T(8,128)} fusion(f32[3,9,64,64]{2,3,0,1:T(8,128)} %fusion.67, bf16[1,64,2,64,256]{4,1,3,2,0:T(8,128)(2,1)S(1)} %copy-done.15, bf16[1,64,2,64,256]{4,1,3,2,0:T(8,128)(2,1)S(1)} %bitcast.549, bf16[1,64,2,64,256]{4,1,3,2,0:T(8,128)(2,1)S(1)} %copy-done.16, bf16[64,2,64,256,1]{3,2,1,0,4:T(8,128)(2,1)} %bitcast.563), kind=kOutput, calls=%fused_computation.115 | convolution fusion | flops 817889280 | bytes 16875520 | tf_op jit(solution)/shard_map/izxy,dozxy->dio/dot_general | solution.py:146
  429.3 6.6 %fusion.15 = f32[2,64,256,64,1]{2,3,1,0,4:T(8,128)} fusion(bf16[1,64,2,64,256]{4,1,3,2,0:T(8,128)(2,1)S(1)} %copy-done.13, bf16[1,64,2,64,256]{4,1,3,2,0:T(8,128)(2,1)} %get-tuple-element.35, bf16[1,64,2,64,256]{4,1,3,2,0:T(8,128)(2,1)S(1)} %copy-done.14, bf16[27,64,64]{2,1,0:T(8,128)(2,1)S(1)} %copy-done.29), kind=kOutput, calls=%fused_computation.39 | convolution fusion | flops 843055104 | bytes 21020672 | tf_op jit(solution)/shard_map/dio,dozxy->izxy/dot_general | solution.py:148
  436.0 10.4 %fusion.79 = f32[3,9,64,64]{2,3,0,1:T(8,128)} fusion(f32[3,9,64,64]{2,3,0,1:T(8,128)} %fusion.73, bf16[1,64,2,64,256]{4,1,3,2,0:T(8,128)(2,1)S(1)} %copy-done.13, bf16[1,64,2,64,256]{4,1,3,2,0:T(8,128)(2,1)} %get-tuple-element.35, bf16[1,64,2,64,256]{4,1,3,2,0:T(8,128)(2,1)S(1)} %copy-done.14, bf16[64,2,64,256,1]{3,2,1,0,4:T(8,128)(2,1)} %bitcast.564), kind=kOutput, calls=%fused_computation.117 | convolution fusion | flops 817889280 | bytes 16875520 | tf_op jit(solution)/shard_map/izxy,dozxy->dio/dot_general | solution.py:146
  451.8 9.3 %fusion.85 = f32[3,9,64,64]{2,3,0,1:T(8,128)} fusion(f32[3,9,64,64]{2,3,0,1:T(8,128)} %fusion.79, bf16[1,64,2,64,256]{4,1,3,2,0:T(8,128)(2,1)S(1)} %copy-done.11, bf16[1,64,2,64,256]{4,1,3,2,0:T(8,128)(2,1)S(1)} %copy-done.24, bf16[1,64,2,64,256]{4,1,3,2,0:T(8,128)(2,1)S(1)} %copy-done.12, bf16[64,2,64,256,1]{3,2,1,0,4:T(8,128)(2,1)} %bitcast.565), kind=kOutput, calls=%fused_computation.119 | convolution fusion | flops 817889280 | bytes 16875520 | tf_op jit(solution)/shard_map/izxy,dozxy->dio/dot_general | solution.py:146
  466.7 9.3 %fusion.91 = f32[3,9,64,64]{2,3,0,1:T(8,128)} fusion(f32[3,9,64,64]{2,3,0,1:T(8,128)} %fusion.85, bf16[1,64,2,64,256]{4,1,3,2,0:T(8,128)(2,1)S(1)} %copy-done.8, bf16[1,64,2,64,256]{4,1,3,2,0:T(8,128)(2,1)S(1)} %copy-done.5, bf16[1,64,2,64,256]{4,1,3,2,0:T(8,128)(2,1)S(1)} %copy-done.9, bf16[64,2,64,256,1]{3,2,1,0,4:T(8,128)(2,1)} %bitcast.566), kind=kOutput, calls=%fused_computation.121 | convolution fusion | flops 817889280 | bytes 16875520 | tf_op jit(solution)/shard_map/izxy,dozxy->dio/dot_general | solution.py:146
  481.3 6.4 %fusion.97 = f32[3,9,64,64]{2,3,0,1:T(8,128)} fusion(f32[3,9,64,64]{2,3,0,1:T(8,128)} %fusion.91, bf16[1,64,2,64,256]{4,1,3,2,0:T(8,128)(2,1)S(1)} %copy-done.7, bf16[1,64,2,64,256]{4,1,3,2,0:T(8,128)(2,1)S(1)} %copy-done.25, bf16[1,64,2,64,256]{4,1,3,2,0:T(8,128)(2,1)S(1)} %copy-done.6, bf16[64,2,64,256,1]{3,2,1,0,4:T(8,128)(2,1)S(1)} %bitcast.567), kind=kOutput, calls=%fused_computation.123 | convolution fusion | flops 817889280 | bytes 16875520 | tf_op jit(solution)/shard_map/izxy,dozxy->dio/dot_general | solution.py:146
  490.1 25.0 %fusion.39 = bf16[64,2,64,256]{3,0,1,2:T(8,128)(2,1)S(1)} fusion(f32[2,64,256,64,1]{2,3,1,0,4:T(8,128)} %fusion.9, f32[2,64,256,64,1]{2,3,1,0,4:T(8,128)} %fusion.11, f32[2,64,256,64,1]{2,3,1,0,4:T(8,128)} %fusion.13, f32[2,64,256,64,1]{2,3,1,0,4:T(8,128)} %fusion.15, f32[2,64,256,64,1]{2,3,1,0,4:T(8,128)} %fusion.17, f32[2,64,256,64,1]{2,3,1,0,4:T(8,128)} %fusion.19, ...), kind=kLoop, calls=%fused_computation.90 | loop fusion | flops 18874368 | bytes 79691776 | tf_op jit(solution)/shard_map/convert_element_type | solution.py:153
  519.6 61.7 %all-reduce.4.cloned.1.call-done = f32[27,64,64]{2,1,0:T(8,128)} async-done(((f32[27,64,64]{2,1,0:T(8,128)}), f32[27,64,64]{2,1,0:T(8,128)}) %all-reduce.4.cloned.1.call-update) | async-done | bytes 442384 | tf_op jit(solution)/shard_map/psum | solution.py:152
  (191 shorter events, 196.1 us)
Async XLA Ops:
  7.2 128.0 %copy-start = (bf16[27,64]{1,0:T(8,128)(2,1)S(1)}, bf16[27,64]{1,0:T(8,128)(2,1)}, u32[]{:S(2)}) copy-start(bf16[27,64]{1,0:T(8,128)(2,1)} %param.13) | copy-start | bytes 10372
  7.2 14.7 %reduce-scatter.4.cloned.1.call-start = ((), (), s32[]{:S(2)}) async-start(), calls=%async_computation.7 | async-start | bytes 393216 | tf_op jit(solution)/shard_map/reduce_scatter | solution.py:64
  11.4 22.3 %reduce-scatter.6.cloned.1.call-start = ((), (), s32[]{:S(2)}) async-start(), calls=%async_computation.8 | async-start | bytes 393216 | tf_op jit(solution)/shard_map/reduce_scatter | solution.py:65
  23.8 13.2 %all-to-all-start = ((f32[8,1,4096]{2,1,0:T(1,128)}), f32[8,1,4096]{2,1,0:T(1,128)S(1)}, u32[]{:S(2)}, u32[]{:S(2)}) async-start(f32[8,1,4096]{2,1,0:T(1,128)} %reshape.165), calls=%async_computation.1 | async-start | bytes 262144 | tf_op jit(solution)/shard_map/all_to_all | solution.py:70
  37.0 12.2 %all-to-all-start.1 = ((f32[8,1,4096]{2,1,0:T(1,128)}), f32[8,1,4096]{2,1,0:T(1,128)S(1)}, u32[]{:S(2)}, u32[]{:S(2)}) async-start(f32[8,1,4096]{2,1,0:T(1,128)} %reshape.167), calls=%async_computation.3 | async-start | bytes 262144 | tf_op jit(solution)/shard_map/all_to_all | solution.py:77
  80.5 12.6 %all-to-all-start.2 = ((f32[8,1,4096]{2,1,0:T(1,128)}), f32[8,1,4096]{2,1,0:T(1,128)S(1)}, u32[]{:S(2)}, u32[]{:S(2)}) async-start(f32[8,1,4096]{2,1,0:T(1,128)} %reshape.169), calls=%async_computation.4 | async-start | bytes 262144 | tf_op jit(solution)/shard_map/all_to_all | solution.py:102
  93.1 11.8 %all-to-all-start.3 = ((f32[8,1,4096]{2,1,0:T(1,128)}), f32[8,1,4096]{2,1,0:T(1,128)S(1)}, u32[]{:S(2)}, u32[]{:S(2)}) async-start(f32[8,1,4096]{2,1,0:T(1,128)} %reshape.171), calls=%async_computation.5 | async-start | bytes 262144 | tf_op jit(solution)/shard_map/all_to_all | solution.py:109
  97.5 19.8 %reduce-scatter.8.cloned.1.call-start = ((), (), s32[]{:S(2)}) async-start(), calls=%async_computation.9 | async-start | bytes 393216 | tf_op jit(solution)/shard_map/reduce_scatter | solution.py:124
  111.7 469.5 %all-reduce.4.cloned.1.call-start = ((), (), s32[]{:S(2)}) async-start(), calls=%async_computation.10 | async-start | bytes 1769472 | tf_op jit(solution)/shard_map/psum | solution.py:152
  117.3 17.8 %copy-start.27 = (bf16[64,2,64,256]{3,2,1,0:T(8,128)(2,1)S(1)}, bf16[64,2,64,256]{3,2,1,0:T(8,128)(2,1)}, u32[]{:S(2)}) copy-start(bf16[64,2,64,256]{3,2,1,0:T(8,128)(2,1)} %param.11) | copy-start | bytes 12582916
  118.4 5.1 collective-permute-start
  122.2 5.5 collective-permute-start.1
  127.8 2.6 collective-permute-start.2
  129.1 3.1 collective-permute-start.3
  141.7 72.4 %collective-permute-start.4 = (bf16[64,2,1,256]{3,0,2,1:T(8,128)(2,1)S(1)}, bf16[64,2,1,256]{3,0,2,1:T(8,128)(2,1)S(1)}, u32[]{:S(2)}, u32[]{:S(2)}) collective-permute-start(bf16[64,2,1,256]{3,0,2,1:T(8,128)(2,1)S(1)} %get-tuple-element.42), channel_id=1, source_target_pairs={{0,2},{2,4},{4,6},{6,8},{8,10},{10,12},{12,14},{1,3},{3,5},{5,7},{... | collective-permute-start | bytes 196616 | tf_op jit(solution)/shard_map/ppermute | solution.py:17
  145.9 68.1 %collective-permute-start.5 = (bf16[64,2,1,256]{3,0,2,1:T(8,128)(2,1)S(1)}, bf16[64,2,1,256]{3,0,2,1:T(8,128)(2,1)S(1)}, u32[]{:S(2)}, u32[]{:S(2)}) collective-permute-start(bf16[64,2,1,256]{3,0,2,1:T(8,128)(2,1)S(1)} %get-tuple-element.43), channel_id=1, source_target_pairs={{2,0},{4,2},{6,4},{8,6},{10,8},{12,10},{14,12},{3,1},{5,3},{7,5},{... | collective-permute-start | bytes 196616 | tf_op jit(solution)/shard_map/ppermute | solution.py:18
  222.6 11.1 %collective-permute-start.6 = (bf16[64,2,66,1]{2,0,3,1:T(8,128)(2,1)S(1)}, bf16[64,2,66,1]{2,0,3,1:T(8,128)(2,1)S(1)}, u32[]{:S(2)}, u32[]{:S(2)}) collective-permute-start(bf16[64,2,66,1]{2,0,3,1:T(8,128)(2,1)S(1)} %copy.101), channel_id=1, source_target_pairs={{0,1},{2,3},{4,5},{6,7},{8,9},{10,11},{12,13},{14,15},{16,17},{18,... | collective-permute-start | bytes 50696 | tf_op jit(solution)/shard_map/ppermute | solution.py:17
  226.4 11.8 %collective-permute-start.7 = (bf16[64,2,66,1]{2,0,3,1:T(8,128)(2,1)S(1)}, bf16[64,2,66,1]{2,0,3,1:T(8,128)(2,1)S(1)}, u32[]{:S(2)}, u32[]{:S(2)}) collective-permute-start(bf16[64,2,66,1]{2,0,3,1:T(8,128)(2,1)S(1)} %copy.102), channel_id=1, source_target_pairs={{1,0},{3,2},{5,4},{7,6},{9,8},{11,10},{13,12},{15,14},{17,16},{19,... | collective-permute-start | bytes 50696 | tf_op jit(solution)/shard_map/ppermute | solution.py:18
  333.2 15.4 %copy-start.29 = (bf16[27,64,64]{2,1,0:T(8,128)(2,1)S(1)}, bf16[27,64,64]{2,1,0:T(8,128)(2,1)}, u32[]{:S(2)}) copy-start(bf16[27,64,64]{2,1,0:T(8,128)(2,1)} %param.12) | copy-start | bytes 663556
  348.6 11.2 %copy-start.22 = (bf16[1,64,2,64,256]{4,1,3,2,0:T(8,128)(2,1)S(1)}, bf16[1,64,2,64,256]{4,1,3,2,0:T(8,128)(2,1)}, u32[]{:S(2)}) copy-start(bf16[1,64,2,64,256]{4,1,3,2,0:T(8,128)(2,1)} %get-tuple-element.27) | copy-start | bytes 12582916
  404.2 10.4 %copy-start.15 = (bf16[1,64,2,64,256]{4,1,3,2,0:T(8,128)(2,1)S(1)}, bf16[1,64,2,64,256]{4,1,3,2,0:T(8,128)(2,1)}, u32[]{:S(2)}) copy-start(bf16[1,64,2,64,256]{4,1,3,2,0:T(8,128)(2,1)} %get-tuple-element.20) | copy-start | bytes 12582916
  435.9 10.5 %copy-start.11 = (bf16[1,64,2,64,256]{4,1,3,2,0:T(8,128)(2,1)S(1)}, bf16[1,64,2,64,256]{4,1,3,2,0:T(8,128)(2,1)}, u32[]{:S(2)}) copy-start(bf16[1,64,2,64,256]{4,1,3,2,0:T(8,128)(2,1)} %get-tuple-element.16) | copy-start | bytes 12582916
  436.0 10.4 %copy-start.12 = (bf16[1,64,2,64,256]{4,1,3,2,0:T(8,128)(2,1)S(1)}, bf16[1,64,2,64,256]{4,1,3,2,0:T(8,128)(2,1)}, u32[]{:S(2)}) copy-start(bf16[1,64,2,64,256]{4,1,3,2,0:T(8,128)(2,1)} %get-tuple-element.17) | copy-start | bytes 12582916
  490.1 93.3 %copy-start.1 = (bf16[27,64]{1,0:T(8,128)(2,1)S(1)}, bf16[27,64]{1,0:T(8,128)(2,1)}, u32[]{:S(2)}) copy-start(bf16[27,64]{1,0:T(8,128)(2,1)} %param.13) | copy-start | bytes 10372
  (23 other events, 189.6 us)
Sparse Core Ops, SparseCore 0:
  11.5 10.3 reduce-scatter.3
  24.8 8.8 reduce-scatter.5
  111.9 5.4 reduce-scatter.7
  490.3 90.9 all-reduce.3
where the time goes:
time: 596 us; the launch traced here: 590 us
  matrix products  207 us (35%)
  local copies, waits for them, and re-layouts  121 us (20%)
  waiting for transfers between devices  93.5 us (16%)
  blocking collectives  60 us (10%)
  other arithmetic  56.7 us (10%)
  starting transfers between devices  36.9 us (6%)
  between operations  14.8 us (2%)
    dot_general x9, matrix products, shards(): jnp.einsum('izxy,dozxy->dio', act_in, stacked, preferred_element_type=jnp...  90.2 us
    another operation x4, local copies, waits for them, and re-layouts, shifted_windows(): return jnp.stack(windows, axis=0)  78.2 us
    psum x1, waiting for transfers between devices, shards(): lax.psum((grad_first, grad_second), ('wide', 'narrow'))  61.7 us
    psum x1, blocking collectives, shards(): lax.psum((grad_first, grad_second), ('wide', 'narrow'))  60 us
    dot_general x9, matrix products, shards(): jnp.einsum('dio,dozxy->izxy', w_first[plane_index::9], stacked, preferred...  53.7 us
    convert_element_type x1, other arithmetic, shards(): return (grad_in.astype(jnp.bfloat16), grad_first, grad_second)  25 us
    concatenate x6, other arithmetic, with_halo(): x = jnp.concatenate([before, x, after], axis=dim)  19.9 us
    unnamed x95, local copies, waits for them, and re-layouts  19.5 us
  transfers between devices with their start and end apart: 16, of which 10 were waited for; matrix products, arithmetic and copies ran while one was open for 12% of the time, Pallas kernels for 0%

commit v1 on v0

--- a/solution.py
+++ b/solution.py
@@ -2,6 +2,7 @@
 import jax.numpy as jnp
 from jax import lax
 from jax.sharding import PartitionSpec as P
+from jax.lax import psum
 
 two_pi = 6.283185307179586
 highest = lax.Precision.HIGHEST
@@ -149,7 +150,7 @@
             "dio,dozxy->izxy", w_first[plane_index::9], stacked, preferred_element_type=jnp.float32
         )
     grad_first = jnp.stack(first_parts, axis=1).reshape(27, channels, channels)
-    grad_first, grad_second = lax.psum((grad_first, grad_second), ("wide", "narrow"))
+    grad_first, grad_second = psum(psum((grad_first, grad_second), "wide"), "narrow")
     return (grad_in.astype(jnp.bfloat16), grad_first, grad_second)
 
 

time: 596 us -> 591 us (level)
  blocking collectives: 60 us -> 39.8 us
  matrix products: 207 us -> 216 us
    psum x1 -> x2, blocking collectives: 60 us -> 39.8 us  [the longest x1 35.9 us: shards(): psum((grad_first, grad_second), 'wide')]
    psum x1 -> x2, waiting for transfers between devices: 61.7 us -> 65.6 us  [the longest x1 65.6 us: shards(): psum((grad_first, grad_second), 'wide')]
  transfers between devices with their start and end apart: 16 -> 17, of which waited for: 10 -> 10; matrix products, arithmetic and copies ran while one was open for 12% -> 13% of each run, Pallas kernels for 0% -> 0%
where the time goes in v1:
time: 591 us; the launch traced here: 586 us
  matrix products  216 us (37%)
  local copies, waits for them, and re-layouts  122 us (21%)
  waiting for transfers between devices  97.5 us (16%)
  other arithmetic  57.2 us (10%)
  blocking collectives  39.8 us (7%)
  starting transfers between devices  37.8 us (6%)
  between operations  14.9 us (3%)
    dot_general x9, matrix products, shards(): jnp.einsum('izxy,dozxy->dio', act_in, stacked, preferred_element_type=jnp...  96.1 us
    another operation x4, local copies, waits for them, and re-layouts, shifted_windows(): return jnp.stack(windows, axis=0)  78.2 us
    psum x1, waiting for transfers between devices, shards(): psum((grad_first, grad_second), 'wide')  65.6 us
    dot_general x9, matrix products, shards(): jnp.einsum('dio,dozxy->izxy', w_first[plane_index::9], stacked, preferred...  56.6 us
    psum x1, blocking collectives, shards(): psum((grad_first, grad_second), 'wide')  35.9 us
    convert_element_type x1, other arithmetic, shards(): return (grad_in.astype(jnp.bfloat16), grad_first, grad_second)  25.6 us
    unnamed x95, local copies, waits for them, and re-layouts  20.2 us
    concatenate x6, other arithmetic, with_halo(): x = jnp.concatenate([before, x, after], axis=dim)  19.9 us
  transfers between devices with their start and end apart: 17, of which 10 were waited for; matrix products, arithmetic and copies ran while one was open for 13% of the time, Pallas kernels for 0%

profile of v1, /device:TPU:0, one launch (start us, length us, event | category | flops | bytes accessed | tf_op | source)
XLA Modules:
  0.0 585.6 jit_solution(13320713795234896540)
XLA Ops:
  15.5 6.4 %reduce-scatter.4.cloned.1.call-done = f32[2,64,256]{2,1,0:T(8,128)} async-done(((f32[2,64,512]{2,1,0:T(8,128)}), f32[2,64,256]{2,1,0:T(8,128)}) %reduce-scatter.4.cloned.1.call-update) | async-done | bytes 131088 | tf_op jit(solution)/shard_map/reduce_scatter | solution.py:65
  99.1 6.0 %all-to-all-done.3 = f32[8,1,4096]{2,1,0:T(1,128)S(1)} async-done(((f32[8,1,4096]{2,1,0:T(1,128)}), f32[8,1,4096]{2,1,0:T(1,128)S(1)}, u32[]{:S(2)}, u32[]{:S(2)}) %all-to-all-start.3) | async-done | bytes 131104 | tf_op jit(solution)/shard_map/all_to_all | solution.py:110
  147.6 6.3 %fusion.100 = f32[27,64]{1,0:T(8,128)S(1)} fusion(bf16[64,2,64,256]{3,2,1,0:T(8,128)(2,1)S(1)} %copy-done.28, bf16[27,2,64,256]{3,2,1,0:T(8,128)(2,1)S(1)} %constant_dynamic-update-slice_fusion), kind=kOutput, calls=%fused_computation.124 | convolution fusion | flops 113246208 | bytes 5970688 | tf_op jit(solution)/shard_map/czxy,tzxy->tc/dot_general | solution.py:135
  154.0 35.9 %psum.30 = f32[27,64]{1,0:T(8,128)S(1)} all-reduce(f32[27,64]{1,0:T(8,128)S(1)} %fusion.100), channel_id=1, replica_groups=mesh['grp'=2,'wide'=8,'narrow'=2] {'wide'}, use_global_device_ids=true, to_apply=%region_5.6 | all-reduce | flops 1728 | bytes 13824 | tf_op jit(solution)/shard_map/psum | solution.py:153
  208.9 5.8 fusion.27
  223.7 8.2 %pad_maximum_fusion.9 = (bf16[64,2,66,257]{3,0,2,1:T(8,128)(2,1)S(1)}, bf16[64,2,66,257]{3,0,2,1:T(8,128)(2,1)S(1)}) fusion(bf16[64,2,66,1]{3,0,2,1:T(8,128)(2,1)} %copy.104, bf16[64,2,1,256]{3,0,2,1:T(8,128)(2,1)S(1)} %collective-permute-done.5, bf16[64,2,64,256]{3,0,2,1:T(8,128)(2,1)} %copy-done.2, bf16[64,2,1,256]{3,0,2,1:T(8,128)(2,1)S(1)} %collective-permute-done.4, ...), kind=kLoop, calls=%fused_computation.30 | loop fusion | flops 34738176 | bytes 13043712 | tf_op jit(solution)/shard_map/concatenate | solution.py:20
  231.9 9.2 %slice_bitcast_fusion.22 = (bf16[1,64,2,64,256]{4,1,3,2,0:T(8,128)(2,1)}, bf16[1,64,2,64,256]{4,1,3,2,0:T(8,128)(2,1)}, bf16[1,64,2,64,256]{4,1,3,2,0:T(8,128)(2,1)}) fusion(bf16[64,2,66,257]{3,0,2,1:T(8,128)(2,1)S(1)} %get-tuple-element.36), kind=kLoop, calls=%fused_computation.77 | loop fusion | bytes 25165824 | tf_op jit(solution)/shard_map/stack | solution.py:44
  241.0 9.0 %select_maximum_fusion = bf16[64,4,66,258]{3,0,2,1:T(8,128)(2,1)} fusion(bf16[64,2,66,1]{3,0,2,1:T(8,128)(2,1)} %copy.104, bf16[64,2,66,1]{3,0,2,1:T(8,128)(2,1)S(1)} %copy-done.4, bf16[64,2,1,256]{3,0,2,1:T(8,128)(2,1)S(1)} %collective-permute-done.5, bf16[64,2,64,256]{3,0,2,1:T(8,128)(2,1)S(1)} %copy-done.3, ...), kind=kLoop, calls=%fused_computation.3 | loop fusion | flops 78465024 | bytes 13077504 | tf_op jit(solution)/shard_map/concatenate | solution.py:20
  250.0 64.1 %slice_bitcast_fusion.23 = (bf16[1,64,2,64,256]{4,1,3,2,0:T(8,128)(2,1)}, bf16[1,64,2,64,256]{4,1,3,2,0:T(8,128)(2,1)}, bf16[1,64,2,64,256]{4,1,3,2,0:T(8,128)(2...) fusion(bf16[64,4,66,258]{3,0,2,1:T(8,128)(2,1)} %select_maximum, ...), kind=kLoop, calls=%fused_computation.78 | loop fusion | bytes 150994944 | tf_op jit(solution)/shard_map/stack | solution.py:44
  314.1 14.6 %fusion.49 = f32[3,9,64,64]{2,3,0,1:T(8,128)S(1)} fusion(bf16[1,64,2,64,256]{4,1,3,2,0:T(8,128)(2,1)} %get-tuple-element.28, bf16[1,64,2,64,256]{4,1,3,2,0:T(8,128)(2,1)} %get-tuple-element.30, bf16[1,64,2,64,256]{4,1,3,2,0:T(8,128)(2,1)} %get-tuple-element.12, bf16[64,2,64,256,1]{3,2,1,0,4:T(8,128)(2,1)} %bitcast.559), kind=kOutput, calls=%fused_computation.107 | convolution fusion | flops 817889280 | bytes 16875520 | tf_op jit(solution)/shard_map/izxy,dozxy->dio/dot_general | solution.py:147
  328.7 8.5 %fusion.25 = f32[2,64,256,64,1]{2,3,1,0,4:T(8,128)} fusion(bf16[1,64,2,64,256]{4,1,3,2,0:T(8,128)(2,1)} %get-tuple-element.28, bf16[1,64,2,64,256]{4,1,3,2,0:T(8,128)(2,1)} %get-tuple-element.30, bf16[1,64,2,64,256]{4,1,3,2,0:T(8,128)(2,1)} %get-tuple-element.12, bf16[27,64,64]{2,1,0:T(8,128)(2,1)S(1)} %copy-done.29), kind=kOutput, calls=%fused_computation.49 | convolution fusion | flops 843055104 | bytes 21020672 | tf_op jit(solution)/shard_map/dio,dozxy->izxy/dot_general | solution.py:149
  345.1 10.0 %fusion.55 = f32[3,9,64,64]{2,3,0,1:T(8,128)S(1)} fusion(f32[3,9,64,64]{2,3,0,1:T(8,128)S(1)} %fusion.49, bf16[1,64,2,64,256]{4,1,3,2,0:T(8,128)(2,1)S(1)} %copy-done.21, bf16[1,64,2,64,256]{4,1,3,2,0:T(8,128)(2,1)S(1)} %copy-done.10, bf16[1,64,2,64,256]{4,1,3,2,0:T(8,128)(2,1)S(1)} %copy-done.22, bf16[64,2,64,256,1]{3,2,1,0,4:T(8,128)(2,1)} %bitcast.560), kind=kOutput, calls=%fused_computation.109 | convolution fusion | flops 817889280 | bytes 16875520 | tf_op jit(solution)/shard_map/izxy,dozxy->dio/dot_general | solution.py:147
  367.9 11.4 %fusion.61 = f32[3,9,64,64]{2,3,0,1:T(8,128)S(1)} fusion(f32[3,9,64,64]{2,3,0,1:T(8,128)S(1)} %fusion.55, bf16[1,64,2,64,256]{4,1,3,2,0:T(8,128)(2,1)S(1)} %copy-done.19, bf16[1,64,2,64,256]{4,1,3,2,0:T(8,128)(2,1)} %copy-done.26, bf16[1,64,2,64,256]{4,1,3,2,0:T(8,128)(2,1)S(1)} %copy-done.20, bf16[64,2,64,256,1]{3,2,1,0,4:T(8,128)(2,1)} %bitcast.561), kind=kOutput, calls=%fused_computation.111 | convolution fusion | flops 817889280 | bytes 16875520 | tf_op jit(solution)/shard_map/izxy,dozxy->dio/dot_general | solution.py:147
  379.3 6.8 %fusion.19 = f32[2,64,256,64,1]{2,3,1,0,4:T(8,128)} fusion(bf16[1,64,2,64,256]{4,1,3,2,0:T(8,128)(2,1)S(1)} %copy-done.17, bf16[1,64,2,64,256]{4,1,3,2,0:T(8,128)(2,1)} %get-tuple-element.32, bf16[1,64,2,64,256]{4,1,3,2,0:T(8,128)(2,1)S(1)} %copy-done.18, bf16[27,64,64]{2,1,0:T(8,128)(2,1)S(1)} %copy-done.29), kind=kOutput, calls=%fused_computation.43 | convolution fusion | flops 843055104 | bytes 21020672 | tf_op jit(solution)/shard_map/dio,dozxy->izxy/dot_general | solution.py:149
  386.1 11.5 %fusion.67 = f32[3,9,64,64]{2,3,0,1:T(8,128)S(1)} fusion(f32[3,9,64,64]{2,3,0,1:T(8,128)S(1)} %fusion.61, bf16[1,64,2,64,256]{4,1,3,2,0:T(8,128)(2,1)S(1)} %copy-done.17, bf16[1,64,2,64,256]{4,1,3,2,0:T(8,128)(2,1)} %get-tuple-element.32, bf16[1,64,2,64,256]{4,1,3,2,0:T(8,128)(2,1)S(1)} %copy-done.18, bf16[64,2,64,256,1]{3,2,1,0,4:T(8,128)(2,1)} %bitcast.562), kind=kOutput, calls=%fused_computation.113 | convolution fusion | flops 817889280 | bytes 16875520 | tf_op jit(solution)/shard_map/izxy,dozxy->dio/dot_general | solution.py:147
  403.0 10.3 %fusion.73 = f32[3,9,64,64]{2,3,0,1:T(8,128)S(1)} fusion(f32[3,9,64,64]{2,3,0,1:T(8,128)S(1)} %fusion.67, bf16[1,64,2,64,256]{4,1,3,2,0:T(8,128)(2,1)S(1)} %copy-done.15, bf16[1,64,2,64,256]{4,1,3,2,0:T(8,128)(2,1)S(1)} %bitcast.549, bf16[1,64,2,64,256]{4,1,3,2,0:T(8,128)(2,1)S(1)} %copy-done.16, bf16[64,2,64,256,1]{3,2,1,0,4:T(8,128)(2,1)} %bitcast.563), kind=kOutput, calls=%fused_computation.115 | convolution fusion | flops 817889280 | bytes 16875520 | tf_op jit(solution)/shard_map/izxy,dozxy->dio/dot_general | solution.py:147
  414.2 6.6 %fusion.15 = f32[2,64,256,64,1]{2,3,1,0,4:T(8,128)} fusion(bf16[1,64,2,64,256]{4,1,3,2,0:T(8,128)(2,1)S(1)} %copy-done.13, bf16[1,64,2,64,256]{4,1,3,2,0:T(8,128)(2,1)} %get-tuple-element.35, bf16[1,64,2,64,256]{4,1,3,2,0:T(8,128)(2,1)S(1)} %copy-done.14, bf16[27,64,64]{2,1,0:T(8,128)(2,1)S(1)} %copy-done.29), kind=kOutput, calls=%fused_computation.39 | convolution fusion | flops 843055104 | bytes 21020672 | tf_op jit(solution)/shard_map/dio,dozxy->izxy/dot_general | solution.py:149
  420.9 10.4 %fusion.79 = f32[3,9,64,64]{2,3,0,1:T(8,128)} fusion(f32[3,9,64,64]{2,3,0,1:T(8,128)} %copy-done.27, bf16[1,64,2,64,256]{4,1,3,2,0:T(8,128)(2,1)S(1)} %copy-done.13, bf16[1,64,2,64,256]{4,1,3,2,0:T(8,128)(2,1)} %get-tuple-element.35, bf16[1,64,2,64,256]{4,1,3,2,0:T(8,128)(2,1)S(1)} %copy-done.14, bf16[64,2,64,256,1]{3,2,1,0,4:T(8,128)(2,1)} %bitcast.564), kind=kOutput, calls=%fused_computation.117 | convolution fusion | flops 817889280 | bytes 16875520 | tf_op jit(solution)/shard_map/izxy,dozxy->dio/dot_general | solution.py:147
  436.6 9.3 %fusion.85 = f32[3,9,64,64]{2,3,0,1:T(8,128)} fusion(f32[3,9,64,64]{2,3,0,1:T(8,128)} %fusion.79, bf16[1,64,2,64,256]{4,1,3,2,0:T(8,128)(2,1)S(1)} %copy-done.11, bf16[1,64,2,64,256]{4,1,3,2,0:T(8,128)(2,1)S(1)} %copy-done.24, bf16[1,64,2,64,256]{4,1,3,2,0:T(8,128)(2,1)S(1)} %copy-done.12, bf16[64,2,64,256,1]{3,2,1,0,4:T(8,128)(2,1)} %bitcast.565), kind=kOutput, calls=%fused_computation.119 | convolution fusion | flops 817889280 | bytes 16875520 | tf_op jit(solution)/shard_map/izxy,dozxy->dio/dot_general | solution.py:147
  451.5 9.3 %fusion.91 = f32[3,9,64,64]{2,3,0,1:T(8,128)} fusion(f32[3,9,64,64]{2,3,0,1:T(8,128)} %fusion.85, bf16[1,64,2,64,256]{4,1,3,2,0:T(8,128)(2,1)S(1)} %copy-done.8, bf16[1,64,2,64,256]{4,1,3,2,0:T(8,128)(2,1)S(1)} %copy-done.5, bf16[1,64,2,64,256]{4,1,3,2,0:T(8,128)(2,1)S(1)} %copy-done.9, bf16[64,2,64,256,1]{3,2,1,0,4:T(8,128)(2,1)} %bitcast.566), kind=kOutput, calls=%fused_computation.121 | convolution fusion | flops 817889280 | bytes 16875520 | tf_op jit(solution)/shard_map/izxy,dozxy->dio/dot_general | solution.py:147
  460.8 9.2 %fusion.97 = f32[3,9,64,64]{2,3,0,1:T(8,128)} fusion(f32[3,9,64,64]{2,3,0,1:T(8,128)} %fusion.91, bf16[1,64,2,64,256]{4,1,3,2,0:T(8,128)(2,1)S(1)} %copy-done.7, bf16[1,64,2,64,256]{4,1,3,2,0:T(8,128)(2,1)S(1)} %copy-done.25, bf16[1,64,2,64,256]{4,1,3,2,0:T(8,128)(2,1)S(1)} %copy-done.6, bf16[64,2,64,256,1]{3,2,1,0,4:T(8,128)(2,1)} %bitcast.567), kind=kOutput, calls=%fused_computation.123 | convolution fusion | flops 817889280 | bytes 16875520 | tf_op jit(solution)/shard_map/izxy,dozxy->dio/dot_general | solution.py:147
  472.6 8.3 %fusion.9 = f32[2,64,256,64,1]{2,3,1,0,4:T(8,128)} fusion(bf16[1,64,2,64,256]{4,1,3,2,0:T(8,128)(2,1)} %get-tuple-element.29, bf16[1,64,2,64,256]{4,1,3,2,0:T(8,128)(2,1)} %get-tuple-element.34, bf16[1,64,2,64,256]{4,1,3,2,0:T(8,128)(2,1)} %get-tuple-element.13, bf16[27,64,64]{2,1,0:T(8,128)(2,1)S(1)} %copy-done.29), kind=kOutput, calls=%fused_computation.33 | convolution fusion | flops 843055104 | bytes 21020672 | tf_op jit(solution)/shard_map/dio,dozxy->izxy/dot_general | solution.py:149
  480.9 65.6 %all-reduce.5.cloned.1.call-done = f32[27,64,64]{2,1,0:T(8,128)} async-done(((f32[27,64,64]{2,1,0:T(8,128)}), f32[27,64,64]{2,1,0:T(8,128)}) %all-reduce.5.cloned.1.call-update) | async-done | bytes 442384 | tf_op jit(solution)/shard_map/psum | solution.py:153
  546.6 25.6 %fusion.39 = bf16[64,2,64,256]{3,0,1,2:T(8,128)(2,1)S(1)} fusion(f32[2,64,256,64,1]{2,3,1,0,4:T(8,128)} %fusion.9, f32[2,64,256,64,1]{2,3,1,0,4:T(8,128)} %fusion.11, f32[2,64,256,64,1]{2,3,1,0,4:T(8,128)} %fusion.13, f32[2,64,256,64,1]{2,3,1,0,4:T(8,128)} %fusion.15, f32[2,64,256,64,1]{2,3,1,0,4:T(8,128)} %fusion.17, f32[2,64,256,64,1]{2,3,1,0,4:T(8,128)} %fusion.19, ...), kind=kLoop, calls=%fused_computation.90 | loop fusion | flops 18874368 | bytes 79691776 | tf_op jit(solution)/shard_map/convert_element_type | solution.py:154
  (195 shorter events, 202.3 us)
Async XLA Ops:
  7.2 128.1 %copy-start = (bf16[27,64]{1,0:T(8,128)(2,1)S(1)}, bf16[27,64]{1,0:T(8,128)(2,1)}, u32[]{:S(2)}) copy-start(bf16[27,64]{1,0:T(8,128)(2,1)} %param.13) | copy-start | bytes 10372
  7.2 14.7 %reduce-scatter.4.cloned.1.call-start = ((), (), s32[]{:S(2)}) async-start(), calls=%async_computation.7 | async-start | bytes 393216 | tf_op jit(solution)/shard_map/reduce_scatter | solution.py:65
  11.4 22.3 %reduce-scatter.6.cloned.1.call-start = ((), (), s32[]{:S(2)}) async-start(), calls=%async_computation.8 | async-start | bytes 393216 | tf_op jit(solution)/shard_map/reduce_scatter | solution.py:66
  23.8 13.2 %all-to-all-start = ((f32[8,1,4096]{2,1,0:T(1,128)}), f32[8,1,4096]{2,1,0:T(1,128)S(1)}, u32[]{:S(2)}, u32[]{:S(2)}) async-start(f32[8,1,4096]{2,1,0:T(1,128)} %reshape.165), calls=%async_computation.1 | async-start | bytes 262144 | tf_op jit(solution)/shard_map/all_to_all | solution.py:71
  37.0 12.0 %all-to-all-start.1 = ((f32[8,1,4096]{2,1,0:T(1,128)}), f32[8,1,4096]{2,1,0:T(1,128)S(1)}, u32[]{:S(2)}, u32[]{:S(2)}) async-start(f32[8,1,4096]{2,1,0:T(1,128)} %reshape.167), calls=%async_computation.3 | async-start | bytes 262144 | tf_op jit(solution)/shard_map/all_to_all | solution.py:78
  80.7 12.6 %all-to-all-start.2 = ((f32[8,1,4096]{2,1,0:T(1,128)}), f32[8,1,4096]{2,1,0:T(1,128)S(1)}, u32[]{:S(2)}, u32[]{:S(2)}) async-start(f32[8,1,4096]{2,1,0:T(1,128)} %reshape.169), calls=%async_computation.4 | async-start | bytes 262144 | tf_op jit(solution)/shard_map/all_to_all | solution.py:103
  93.2 11.8 %all-to-all-start.3 = ((f32[8,1,4096]{2,1,0:T(1,128)}), f32[8,1,4096]{2,1,0:T(1,128)S(1)}, u32[]{:S(2)}, u32[]{:S(2)}) async-start(f32[8,1,4096]{2,1,0:T(1,128)} %reshape.171), calls=%async_computation.5 | async-start | bytes 262144 | tf_op jit(solution)/shard_map/all_to_all | solution.py:110
  97.7 19.8 %reduce-scatter.8.cloned.1.call-start = ((), (), s32[]{:S(2)}) async-start(), calls=%async_computation.9 | async-start | bytes 393216 | tf_op jit(solution)/shard_map/reduce_scatter | solution.py:125
  111.9 434.6 %all-reduce.5.cloned.1.call-start = ((), (), s32[]{:S(2)}) async-start(), calls=%async_computation.10 | async-start | bytes 1769472 | tf_op jit(solution)/shard_map/psum | solution.py:153
  117.5 17.8 %copy-start.28 = (bf16[64,2,64,256]{3,2,1,0:T(8,128)(2,1)S(1)}, bf16[64,2,64,256]{3,2,1,0:T(8,128)(2,1)}, u32[]{:S(2)}) copy-start(bf16[64,2,64,256]{3,2,1,0:T(8,128)(2,1)} %param.11) | copy-start | bytes 12582916
  118.6 5.0 collective-permute-start
  122.4 5.5 collective-permute-start.1
  127.9 2.6 collective-permute-start.2
  129.2 3.1 collective-permute-start.3
  141.8 52.0 %collective-permute-start.4 = (bf16[64,2,1,256]{3,0,2,1:T(8,128)(2,1)S(1)}, bf16[64,2,1,256]{3,0,2,1:T(8,128)(2,1)S(1)}, u32[]{:S(2)}, u32[]{:S(2)}) collective-permute-start(bf16[64,2,1,256]{3,0,2,1:T(8,128)(2,1)S(1)} %get-tuple-element.42), channel_id=1, source_target_pairs={{0,2},{2,4},{4,6},{6,8},{8,10},{10,12},{12,14},{1,3},{3,5},{5,7},{... | collective-permute-start | bytes 196616 | tf_op jit(solution)/shard_map/ppermute | solution.py:18
  146.1 47.7 %collective-permute-start.5 = (bf16[64,2,1,256]{3,0,2,1:T(8,128)(2,1)S(1)}, bf16[64,2,1,256]{3,0,2,1:T(8,128)(2,1)S(1)}, u32[]{:S(2)}, u32[]{:S(2)}) collective-permute-start(bf16[64,2,1,256]{3,0,2,1:T(8,128)(2,1)S(1)} %get-tuple-element.43), channel_id=1, source_target_pairs={{2,0},{4,2},{6,4},{8,6},{10,8},{12,10},{14,12},{3,1},{5,3},{7,5},{... | collective-permute-start | bytes 196616 | tf_op jit(solution)/shard_map/ppermute | solution.py:19
  202.4 12.3 %collective-permute-start.6 = (bf16[64,2,66,1]{2,0,3,1:T(8,128)(2,1)S(1)}, bf16[64,2,66,1]{2,0,3,1:T(8,128)(2,1)S(1)}, u32[]{:S(2)}, u32[]{:S(2)}) collective-permute-start(bf16[64,2,66,1]{2,0,3,1:T(8,128)(2,1)S(1)} %copy.101), channel_id=1, source_target_pairs={{0,1},{2,3},{4,5},{6,7},{8,9},{10,11},{12,13},{14,15},{16,17},{18,... | collective-permute-start | bytes 50696 | tf_op jit(solution)/shard_map/ppermute | solution.py:18
  207.2 12.0 %collective-permute-start.7 = (bf16[64,2,66,1]{2,0,3,1:T(8,128)(2,1)S(1)}, bf16[64,2,66,1]{2,0,3,1:T(8,128)(2,1)S(1)}, u32[]{:S(2)}, u32[]{:S(2)}) collective-permute-start(bf16[64,2,66,1]{2,0,3,1:T(8,128)(2,1)S(1)} %copy.102), channel_id=1, source_target_pairs={{1,0},{3,2},{5,4},{7,6},{9,8},{11,10},{13,12},{15,14},{17,16},{19,... | collective-permute-start | bytes 50696 | tf_op jit(solution)/shard_map/ppermute | solution.py:19
  314.1 14.6 %copy-start.29 = (bf16[27,64,64]{2,1,0:T(8,128)(2,1)S(1)}, bf16[27,64,64]{2,1,0:T(8,128)(2,1)}, u32[]{:S(2)}) copy-start(bf16[27,64,64]{2,1,0:T(8,128)(2,1)} %param.12) | copy-start | bytes 663556
  367.9 11.4 %copy-start.17 = (bf16[1,64,2,64,256]{4,1,3,2,0:T(8,128)(2,1)S(1)}, bf16[1,64,2,64,256]{4,1,3,2,0:T(8,128)(2,1)}, u32[]{:S(2)}) copy-start(bf16[1,64,2,64,256]{4,1,3,2,0:T(8,128)(2,1)} %get-tuple-element.22) | copy-start | bytes 12582916
  386.1 11.5 %copy-start.15 = (bf16[1,64,2,64,256]{4,1,3,2,0:T(8,128)(2,1)S(1)}, bf16[1,64,2,64,256]{4,1,3,2,0:T(8,128)(2,1)}, u32[]{:S(2)}) copy-start(bf16[1,64,2,64,256]{4,1,3,2,0:T(8,128)(2,1)} %get-tuple-element.20) | copy-start | bytes 12582916
  386.1 11.5 %copy-start.16 = (bf16[1,64,2,64,256]{4,1,3,2,0:T(8,128)(2,1)S(1)}, bf16[1,64,2,64,256]{4,1,3,2,0:T(8,128)(2,1)}, u32[]{:S(2)}) copy-start(bf16[1,64,2,64,256]{4,1,3,2,0:T(8,128)(2,1)} %get-tuple-element.21) | copy-start | bytes 12582916
  472.6 104.1 %all-reduce.7.cloned.1.call-start = ((), (), s32[]{:S(2)}) async-start(), calls=%async_computation.11 | async-start | bytes 1769472 | tf_op jit(solution)/shard_map/psum | solution.py:153
  546.6 32.3 %copy-start.1 = (bf16[27,64]{1,0:T(8,128)(2,1)S(1)}, bf16[27,64]{1,0:T(8,128)(2,1)}, u32[]{:S(2)}) copy-start(bf16[27,64]{1,0:T(8,128)(2,1)} %param.13) | copy-start | bytes 10372
  (24 other events, 201.2 us)
Sparse Core Ops, SparseCore 0:
  11.5 10.3 reduce-scatter.3
  24.8 8.8 reduce-scatter.5
  112.0 5.4 reduce-scatter.7
  472.7 73.7 all-reduce.4
  548.9 18.5 all-reduce.6
